TPU v7x, 32 devices: a whole 2x2x4 slice. The times are simulated.
32 devices in a mesh: row: 4 (over y, x), col: 8 (over z, core).
Axes of the slice: x: 2, y: 2, z: 4, core: 2. Of those that a mesh axis runs over, the one named last changes fastest.
Arguments:
- mode_profiles: bfloat16 [32768, 2048], P(('row', 'col')), may hold values from -0.032958984 to 0.032958984
- region_labels: int32 [32768], P(('row', 'col')), may hold values from 0 to 15
- gain_table: float32 [16], replicated, may hold values from 0.25 to 2
- index_table: float32 [16], replicated, may hold values from -2 to 2
- field_in: bfloat16 [2048, 2048], P('row', 'col'), may hold values from -2 to 2
Outputs:
- field_out: bfloat16 [2048, 2048], P('row', 'col')
All inputs are finite; a program needn't handle non-finite values.
Results may differ from a plain program's by a relative error of at most 0.02.
Values may be sent and summed in bfloat16 or wider, within the bound.
A program may use at most 64 MiB of HBM per device.

v0:
```python
import jax
import jax.numpy as jnp
from jax import lax
from jax.sharding import PartitionSpec as P

TERMS = 6


def on_device(mode_profiles, region_labels, gain_table, index_table, field_in):
    table = gain_table + index_table
    regions = jnp.arange(table.shape[0], dtype=jnp.int32)
    weight = jnp.sum(
        jnp.where(region_labels[:, None] == regions[None, :], table[None, :], 0.0), axis=1
    )
    scaled = (mode_profiles.astype(jnp.float32) * weight[:, None]).astype(jnp.bfloat16)
    strip = lax.psum_scatter(
        lax.dot_general(
            mode_profiles, scaled, (((0,), (0,)), ((), ())), preferred_element_type=jnp.float32
        ).astype(jnp.bfloat16),
        "row",
        scatter_dimension=0,
        tiled=True,
    )
    tile = lax.psum_scatter(strip, "col", scatter_dimension=1, tiled=True).astype(jnp.float32)
    panel = lax.all_gather(tile.astype(jnp.bfloat16), "col", axis=1, tiled=True)
    start_field = field_in.astype(jnp.float32)

    def accumulate(piece):
        return jnp.dot(panel, piece, preferred_element_type=jnp.float32)

    def horner_step(index, carry):
        order = (TERMS - index).astype(jnp.float32)
        product = accumulate(lax.all_gather(carry, "row", axis=0, tiled=True))
        return (start_field + product / order).astype(jnp.bfloat16)

    return lax.fori_loop(0, TERMS, horner_step, field_in)


def solution(mesh):
    return jax.shard_map(
        on_device,
        mesh=mesh,
        in_specs=(P(("row", "col"), None), P(("row", "col")), P(), P(), P("row", "col")),
        out_specs=P("row", "col"),
        check_vma=False,
    )
```

profile of v0, /device:TPU:16, one launch (start us, length us, event | category | flops | bytes accessed | tf_op | source)
XLA Modules:
  0.0 373.8 jit_solution(6159234866059131426)
XLA Ops:
  6.5 0.9 copy.16
  7.5 0.7 add.30
  8.2 0.8 select_reduce_fusion
  8.9 14.2 %convert_bitcast_fusion = bf16[2048,2048]{0,1:T(8,128)(2,1)} fusion(bf16[1024,2048]{1,0:T(8,128)(2,1)} %param.7, f32[1024]{0:T(1024)S(1)} %select_reduce_fusion), kind=kOutput, calls=%fused_computation.3 | convolution fusion | flops 8600420352 | bytes 12587008 | tf_op jit(solution)/shard_map/dot_general | solution.py:17
  23.1 0.0 reduce-scatter.3.cloned.1.call-update
  23.2 0.0 reduce-scatter.5.cloned.1.call-start
  23.2 87.5 %reduce-scatter.3.cloned.1.call-done = bf16[512,2048]{0,1:T(8,128)(2,1)} async-done(((bf16[2048,2048]{0,1:T(8,128)(2,1)}), bf16[512,2048]{0,1:T(8,128)(2,1)}) %reduce-scatter.3.cloned.1.call-update) | async-done | bytes 2097168 | tf_op jit(solution)/shard_map/reduce_scatter | solution.py:16
  110.7 0.0 reduce-scatter.5.cloned.1.call-update
  110.7 0.0 all-gather.3.cloned.1.call-start
  110.8 32.0 %reduce-scatter.5.cloned.1.call-done = bf16[512,256]{0,1:T(8,128)(2,1)} async-done(((bf16[512,2048]{0,1:T(8,128)(2,1)}), bf16[512,256]{0,1:T(8,128)(2,1)}) %reduce-scatter.5.cloned.1.call-update) | async-done | bytes 262160 | tf_op jit(solution)/shard_map/reduce_scatter | solution.py:24
  142.8 0.0 all-gather.3.cloned.1.call-update
  142.9 34.7 %all-gather.3.cloned.1.call-done = bf16[512,2048]{0,1:T(8,128)(2,1)} async-done(((bf16[512,256]{0,1:T(8,128)(2,1)}), bf16[512,2048]{0,1:T(8,128)(2,1)}) %all-gather.3.cloned.1.call-update) | async-done | bytes 2097168 | tf_op jit(solution)/shard_map/all_gather | solution.py:25
  177.6 2.9 copy.7
  180.6 186.0 %while.13 = (s32[]{:T(128)}, bf16[512,256]{1,0:T(8,128)(2,1)S(1)}, bf16[512,2048]{1,0:T(8,128)(2,1)S(1)}, f32[512,256]{1,0:T(8,128)S(1)}, s32[]{:T(128)}, /*index=5*/s32[]{:T(128)}) while((s32[]{:T(128)}, bf16[512,256]{1,0:T(8,128)(2,1)S(1)}, bf16[512,2048]{1,0:T(8,128)(2,1)S(1)}, f32[512,256]{1,0:T(8,128)S(1)}, s32[]{:T(128)}, ...), condition=%wide.region_4.5_spmd, body=%wide.region_3.4_spmd.sunk | while | flops 537264128 | bytes 8913065 | solution.py:36
  180.6 0.0 copy-start
  180.6 0.0 all-gather.5.cloned.1.call-start
  180.6 0.6 copy-done
  181.3 0.0 all-gather.5.cloned.1.call-update
  181.3 28.2 %all-gather.5.cloned.1.call-done = bf16[2048,256]{1,0:T(8,128)(2,1)} async-done(((bf16[512,256]{1,0:T(8,128)(2,1)}), bf16[2048,256]{1,0:T(8,128)(2,1)}) %all-gather.5.cloned.1.call-update) | async-done | bytes 1048592 | tf_op jit(solution)/shard_map/while/body/eval_jaxpr/all_gather | solution.py:33
  209.5 1.9 fusion.11
  211.4 0.0 all-gather.5.cloned.1.call-start
  211.5 0.6 copy-done
  212.1 0.0 all-gather.5.cloned.1.call-update
  212.2 28.2 %all-gather.5.cloned.1.call-done = bf16[2048,256]{1,0:T(8,128)(2,1)} async-done(((bf16[512,256]{1,0:T(8,128)(2,1)}), bf16[2048,256]{1,0:T(8,128)(2,1)}) %all-gather.5.cloned.1.call-update) | async-done | bytes 1048592 | tf_op jit(solution)/shard_map/while/body/eval_jaxpr/all_gather | solution.py:33
  240.3 1.9 fusion.11
  242.3 0.0 all-gather.5.cloned.1.call-start
  242.3 0.6 copy-done
  243.0 0.0 all-gather.5.cloned.1.call-update
  243.0 28.1 %all-gather.5.cloned.1.call-done = bf16[2048,256]{1,0:T(8,128)(2,1)} async-done(((bf16[512,256]{1,0:T(8,128)(2,1)}), bf16[2048,256]{1,0:T(8,128)(2,1)}) %all-gather.5.cloned.1.call-update) | async-done | bytes 1048592 | tf_op jit(solution)/shard_map/while/body/eval_jaxpr/all_gather | solution.py:33
  271.2 1.9 fusion.11
  273.1 0.0 all-gather.5.cloned.1.call-start
  273.2 0.6 copy-done
  273.8 0.1 all-gather.5.cloned.1.call-update
  273.9 28.4 %all-gather.5.cloned.1.call-done = bf16[2048,256]{1,0:T(8,128)(2,1)} async-done(((bf16[512,256]{1,0:T(8,128)(2,1)}), bf16[2048,256]{1,0:T(8,128)(2,1)}) %all-gather.5.cloned.1.call-update) | async-done | bytes 1048592 | tf_op jit(solution)/shard_map/while/body/eval_jaxpr/all_gather | solution.py:33
  302.3 1.9 fusion.11
  304.3 0.0 copy-start
  304.3 0.0 all-gather.5.cloned.1.call-start
  304.3 0.6 copy-done
  305.0 0.1 all-gather.5.cloned.1.call-update
  305.0 28.4 %all-gather.5.cloned.1.call-done = bf16[2048,256]{1,0:T(8,128)(2,1)} async-done(((bf16[512,256]{1,0:T(8,128)(2,1)}), bf16[2048,256]{1,0:T(8,128)(2,1)}) %all-gather.5.cloned.1.call-update) | async-done | bytes 1048592 | tf_op jit(solution)/shard_map/while/body/eval_jaxpr/all_gather | solution.py:33
  333.5 1.9 fusion.11
  335.4 0.0 all-gather.5.cloned.1.call-start
  335.5 0.6 copy-done
  336.1 0.0 all-gather.5.cloned.1.call-update
  336.2 28.4 %all-gather.5.cloned.1.call-done = bf16[2048,256]{1,0:T(8,128)(2,1)} async-done(((bf16[512,256]{1,0:T(8,128)(2,1)}), bf16[2048,256]{1,0:T(8,128)(2,1)}) %all-gather.5.cloned.1.call-update) | async-done | bytes 1048592 | tf_op jit(solution)/shard_map/while/body/eval_jaxpr/all_gather | solution.py:33
  364.6 1.9 fusion.11
  366.6 0.0 copy-start.1
  366.6 0.7 copy-done.1
  (6 shorter events, 0.1 us)
Async XLA Ops:
  6.5 104.2 %reduce-scatter.3.cloned.1.call-start = ((), (), s32[]{:S(2)}) async-start(), calls=%async_computation.2 | async-start | bytes 10485760 | tf_op jit(solution)/shard_map/reduce_scatter | solution.py:16
  23.2 119.6 %reduce-scatter.5.cloned.1.call-start = ((), (), s32[]{:S(2)}) async-start(), calls=%async_computation.3 | async-start | bytes 2359296 | tf_op jit(solution)/shard_map/reduce_scatter | solution.py:24
  110.7 66.9 %all-gather.3.cloned.1.call-start = ((), (), s32[]{:S(2)}) async-start(), calls=%async_computation.4 | async-start | bytes 2359296 | tf_op jit(solution)/shard_map/all_gather | solution.py:25
  180.6 0.7 copy-start
  180.6 28.9 %all-gather.5.cloned.1.call-start = ((), (), s32[]{:S(2)}) async-start(), calls=%async_computation.5 | async-start | bytes 1310720 | tf_op jit(solution)/shard_map/while/body/eval_jaxpr/all_gather | solution.py:33
  211.4 0.7 copy-start
  211.4 28.9 %all-gather.5.cloned.1.call-start = ((), (), s32[]{:S(2)}) async-start(), calls=%async_computation.5 | async-start | bytes 1310720 | tf_op jit(solution)/shard_map/while/body/eval_jaxpr/all_gather | solution.py:33
  242.3 0.7 copy-start
  242.3 28.9 %all-gather.5.cloned.1.call-start = ((), (), s32[]{:S(2)}) async-start(), calls=%async_computation.5 | async-start | bytes 1310720 | tf_op jit(solution)/shard_map/while/body/eval_jaxpr/all_gather | solution.py:33
  273.1 0.7 copy-start
  273.1 29.2 %all-gather.5.cloned.1.call-start = ((), (), s32[]{:S(2)}) async-start(), calls=%async_computation.5 | async-start | bytes 1310720 | tf_op jit(solution)/shard_map/while/body/eval_jaxpr/all_gather | solution.py:33
  304.3 0.7 copy-start
  304.3 29.2 %all-gather.5.cloned.1.call-start = ((), (), s32[]{:S(2)}) async-start(), calls=%async_computation.5 | async-start | bytes 1310720 | tf_op jit(solution)/shard_map/while/body/eval_jaxpr/all_gather | solution.py:33
  335.4 0.7 copy-start
  335.4 29.2 %all-gather.5.cloned.1.call-start = ((), (), s32[]{:S(2)}) async-start(), calls=%async_computation.5 | async-start | bytes 1310720 | tf_op jit(solution)/shard_map/while/body/eval_jaxpr/all_gather | solution.py:33
  366.6 0.7 copy-start.1
Sparse Core Ops, SparseCore 0:
  23.3 87.3 reduce-scatter.2
  113.0 29.7 reduce-scatter.4
  144.4 33.1 all-gather.2
  182.9 26.4 all-gather.4
  213.8 26.4 all-gather.4
  244.6 26.4 all-gather.4
  275.8 26.4 all-gather.4
  306.9 26.4 all-gather.4
  338.1 26.4 all-gather.4
where the time goes:
time: 376 us; the launch traced here: 374 us
  waiting for transfers between devices  324 us (86%)
  matrix products  25.8 us (7%)
  between operations  13.1 us (3%)
  local copies, waits for them, and re-layouts  8.46 us (2%)
    all_gather x6, waiting for transfers between devices, horner_step(): product = accumulate(lax.all_gather(carry, 'row', axis=0, tiled=True))  170 us
    reduce_scatter x1, waiting for transfers between devices, on_device(): lax.psum_scatter(lax.dot_general(mode_profiles, scaled, (((0,), (0,)), ((...  87.5 us
    all_gather x1, waiting for transfers between devices, on_device(): panel = lax.all_gather(tile.astype(jnp.bfloat16), 'col', axis=1, tiled=True)  34.7 us
    reduce_scatter x1, waiting for transfers between devices, on_device(): lax.psum_scatter(strip, 'col', scatter_dimension=1, tiled=True)  32 us
    dot_general x1, matrix products, on_device(): lax.dot_general(mode_profiles, scaled, (((0,), (0,)), ((), ())), preferre...  14.2 us
    dot_general x6, matrix products, accumulate(): return jnp.dot(panel, piece, preferred_element_type=jnp.float32)  11.6 us
  transfers between devices with their start and end apart: 9, of which 9 were waited for; matrix products, arithmetic and copies ran while one was open for 0% of the time, Pallas kernels for 0%

commit v1 on v0

v1 whole, which is shorter than its diff:
```python
import functools

import jax
import jax.numpy as jnp
from jax import lax
from jax.experimental import pallas as pl
from jax.experimental.pallas import tpu as pltpu
from jax.sharding import PartitionSpec as P

TERMS = 6
LANES = 128
MESH = pl.DeviceIdType.MESH


def lowest_bit(g):
    t = 0
    while not (g >> t) & 1:
        t += 1
    return t


def kernel(R, Z, n, p_ref, w_ref, f_ref, out_ref, s2, part, r0, rt, rz, cx, x0, xs, ot, send_sem, recv_sem):
    bits = R.bit_length() - 1
    blocks = n // LANES
    half = blocks // 2
    width = (half + 1) * LANES
    depth = n // (R * Z * 2)
    mine_cols = x0.shape[0]
    row_rows = n // R
    row, col = lax.axis_index("row"), lax.axis_index("col")
    z, h = col // 2, col % 2
    partner = (row, z * 2 + 1 - h)

    def flip(r, t):
        mask0, mask1 = 1 << t, 1 << (bits - 1 - t)
        mask = mask0 + h * (mask1 - mask0)
        return r + mask * (1 - 2 * ((r // mask) % 2))

    def row_of(g):
        r = row
        for t in range(bits):
            if (g >> t) & 1:
                r = flip(r, t)
        return r

    def mirrored(g):
        return sum(((g >> t) & 1) << (bits - 1 - t) for t in range(bits))

    def z_of(j):
        return (z + 1 + j) % Z

    def strip_of(r, zz, hh):
        return (r * Z + zz) * 2 + hh

    def rows_of(ref, s):
        return ref.at[pl.ds(pl.multiple_of(s * depth, depth), depth), :]

    def window_of(s):
        start = pl.multiple_of((s * depth // LANES) * LANES, LANES)
        return cx.at[pl.ds(pl.multiple_of(s * depth, depth), depth), pl.ds(start, width)]

    ids, started = {}, []

    def slot(key):
        return ids.setdefault(key, len(ids))

    def send(src, dst, device, key):
        copy = pltpu.make_async_remote_copy(
            src_ref=src, dst_ref=dst, send_sem=send_sem.at[len(started)],
            recv_sem=recv_sem.at[slot(key)], device_id=device, device_id_type=MESH)
        copy.start()
        started.append(copy)

    def arrived(ref, key):
        pltpu.make_async_remote_copy(
            src_ref=ref, dst_ref=ref, send_sem=send_sem.at[0],
            recv_sem=recv_sem.at[slot(key)], device_id=partner, device_id_type=MESH).wait_recv()

    barrier = pltpu.get_barrier_semaphore()
    peers = [((row + k) % R, col) for k in range(1, R)]
    peers += [(row, ((z + k) % Z) * 2 + h) for k in range(1, Z)] + [partner]
    for peer in peers:
        pl.semaphore_signal(barrier, inc=1, device_id=peer, device_id_type=MESH)
    pl.semaphore_wait(barrier, len(peers))

    def columns_at(r):
        return pl.ds(pl.multiple_of(r * row_rows, row_rows), row_rows)

    def slab_at(r):
        return pl.ds(pl.multiple_of(r * mine_cols, mine_cols), mine_cols)

    for k in range(1, R):
        to = (row + k) % R
        send(f_ref.at[slab_at(to), :], x0.at[:, columns_at(row)], (to, col), ("field", k))
    x0[:, columns_at(row)] = f_ref[slab_at(row), :]

    scaled = (p_ref[...].astype(jnp.float32) * w_ref[...]).astype(jnp.bfloat16)
    s2[:, :n] = scaled
    s2[:, n:] = scaled[:, : width - LANES]

    order = sorted(range(R), key=lambda g: (lowest_bit(g) if g else bits, -g))
    pair = 2 * LANES
    for g in order:
        r = row_of(g)

        @pl.loop(0, row_rows // pair)
        def _(q):
            base = pl.multiple_of(r * row_rows + q * pair, pair)
            left = p_ref[:, pl.ds(base, pair)].T
            both = jnp.dot(left, s2[:, pl.ds(base, width + LANES)], preferred_element_type=jnp.float32)
            part[pl.ds(base, LANES), :] = both[:LANES, :width].astype(jnp.bfloat16)
            part[pl.ds(base + LANES, LANES), :] = both[LANES:, LANES:].astype(jnp.bfloat16)

        for j in range(Z):
            send(rows_of(part, strip_of(r, z_of(j), 1 - h)), r0.at[mirrored(g) * Z + j], partner, ("core", mirrored(g), j))
            ids.setdefault(("core", g, j), len(ids))

    stage_slot = {}
    for t in range(bits):
        for g in range(R):
            if g % (2 << t) == 0:
                stage_slot[t, g] = len(stage_slot)

    for g in order:
        r = row_of(g)
        low = lowest_bit(g) if g else bits
        for j in range(Z):
            arrived(r0.at[g * Z + j], ("core", g, j))
            own = rows_of(part, strip_of(r, z_of(j), h))
            total = own[...].astype(jnp.float32) + r0[g * Z + j].astype(jnp.float32)
            for t in range(low):
                piece = rt.at[stage_slot[t, g] * Z + j]
                arrived(piece, ("row", t, g, j))
                total = total + piece[...].astype(jnp.float32)
            if g:
                own[...] = total.astype(jnp.bfloat16)
                seen = g ^ (1 << low)
                send(own, rt.at[stage_slot[low, seen] * Z + j], (flip(row, low), col), ("row", low, seen, j))
            elif j < Z - 1:
                own[...] = total.astype(jnp.bfloat16)
                send(own, rz.at[j], (row, z_of(j) * 2 + h), ("z", j))
            else:
                for i in range(Z - 1):
                    arrived(rz.at[i], ("z", i))
                    total = total + rz[i].astype(jnp.float32)
                window_of(strip_of(row, z, h))[...] = total.astype(jnp.bfloat16)

    def spread(g, strip, key_j):
        low = lowest_bit(g) if g else bits
        view = window_of(strip)
        for t in reversed(range(low)):
            send(view, view, (flip(row, t), col), ("spread", g | (1 << t), key_j))
        send(view, view, partner, ("spread_core", mirrored(g), key_j))

    mine = window_of(strip_of(row, z, h))
    for j in range(Z - 1):
        send(mine, mine, (row, z_of(j) * 2 + h), ("spread", 0, j + 1))
    for j in range(Z):
        for g in range(R):
            low = lowest_bit(g) if g else bits
            source_z = (z + Z - j) % Z
            strip = strip_of(row_of(g), source_z, h)
            if g or j:
                arrived(window_of(strip), ("spread", g, j))
            spread(g, strip, j)
    for j in range(Z):
        for g in range(R):
            strip = strip_of(row_of(g), (z + Z - j) % Z, 1 - h)
            arrived(window_of(strip), ("spread_core", g, j))

    @pl.loop(0, blocks)
    def _(i):
        rows = pl.ds(pl.multiple_of(i * LANES, LANES), LANES)

        for d in range(1, half):
            to = pl.multiple_of(((i + d) % blocks) * LANES, LANES)
            block = cx[rows, pl.ds(pl.multiple_of((i + d) * LANES, LANES), LANES)]
            cx[pl.ds(to, LANES), rows] = block.T

    for i in range(half, blocks):
        rows = pl.ds(i * LANES, LANES)
        over = (i + half + 1 - blocks) * LANES
        cx[rows, :over] = cx[rows, n : n + over]

    for k in range(1, R):
        arrived(x0.at[:, columns_at((row + R - k) % R)], ("field", k))
    chunk = 4 * LANES
    for index in range(TERMS):
        source = x0 if index == 0 else xs.at[(index + 1) % 2]
        target = xs.at[index % 2]
        scale = 1.0 / (TERMS - index)

        @pl.loop(0, n // chunk)
        def _(c):
            columns = pl.ds(pl.multiple_of(c * chunk, chunk), chunk)
            product = jnp.dot(source[...], cx[:, columns], preferred_element_type=jnp.float32)
            target[:, columns] = (x0[:, columns].astype(jnp.float32) + scale * product).astype(jnp.bfloat16)

    last = xs.at[(TERMS - 1) % 2]
    for k in range(1, R):
        to = (row + k) % R
        send(last.at[:, columns_at(to)], ot.at[slab_at(row), :], (to, col), ("out", k))
    out_ref[slab_at(row), :] = last[:, columns_at(row)]
    for k in range(1, R):
        source = slab_at((row + R - k) % R)
        arrived(ot.at[source, :], ("out", k))
        out_ref[source, :] = ot[source, :]
    for copy in started:
        copy.wait_send()


def on_device(R, Z, mode_profiles, region_labels, gain_table, index_table, field_in):
    table = gain_table + index_table
    regions = jnp.arange(table.shape[0], dtype=jnp.int32)
    weight = jnp.sum(
        jnp.where(region_labels[:, None] == regions[None, :], table[None, :], 0.0), axis=1, keepdims=True
    )
    points, n = mode_profiles.shape
    width = n // 2 + LANES
    depth = n // (R * Z * 2)
    mine_cols = field_in.shape[1] // R
    messages = 2 * R * Z + 2 * (R - 1) * Z + 2 * (Z - 1) + 2 * (R - 1)
    bf16 = jnp.bfloat16
    turned = pl.pallas_call(
        functools.partial(kernel, R, Z, n),
        out_shape=jax.ShapeDtypeStruct(field_in.shape[::-1], bf16),
        in_specs=[pl.BlockSpec(memory_space=pltpu.VMEM)] * 3,
        out_specs=pl.BlockSpec(memory_space=pltpu.VMEM),
        scratch_shapes=[
            pltpu.VMEM((points, n + width - LANES), bf16),
            pltpu.VMEM((n, width), bf16),
            pltpu.VMEM((R * Z, depth, width), bf16),
            pltpu.VMEM(((R - 1) * Z, depth, width), bf16),
            pltpu.VMEM((Z - 1, depth, width), bf16),
            pltpu.VMEM((n, n + width - LANES), bf16),
            pltpu.VMEM((mine_cols, n), bf16),
            pltpu.VMEM((2, mine_cols, n), bf16),
            pltpu.VMEM(field_in.shape[::-1], bf16),
            pltpu.SemaphoreType.DMA((messages,)),
            pltpu.SemaphoreType.DMA((messages,)),
        ],
        compiler_params=pltpu.CompilerParams(
            collective_id=0, has_side_effects=True, vmem_limit_bytes=60 * 1024 * 1024),
    )(mode_profiles, weight, field_in.T)
    return turned.T


def solution(mesh):
    return jax.shard_map(
        functools.partial(on_device, mesh.shape["row"], mesh.shape["col"] // 2),
        mesh=mesh,
        in_specs=(P(("row", "col"), None), P(("row", "col")), P(), P(), P("row", "col")),
        out_specs=P("row", "col"),
        check_vma=False,
    )
```

time: 376 us -> 118 us (0.31)
  the two profiles are of different devices: /device:TPU:16 before, /device:TPU:9 now
where the time goes in v1:
time: 118 us
  Pallas kernels  112 us (95%)
  local copies, waits for them, and re-layouts  4.61 us (4%)
  other arithmetic  1.44 us (1%)
    pallas_call x1, Pallas kernels, on_device(): pl.pallas_call(functools.partial(kernel, R, Z, n), out_shape=jax.ShapeDty...  112 us

profile of v1, /device:TPU:9, one launch (start us, length us, event | category | flops | bytes accessed | tf_op | source)
XLA Modules:
  0.0 117.8 jit_solution(11797046425442430314)
XLA Ops:
  0.0 0.7 add.3
  0.7 0.8 select_reduce_fusion
  1.4 1.8 %copy.11 = bf16[512,256]{0,1:T(8,128)(2,1)} copy(bf16[512,256]{1,0:T(8,128)(2,1)} %param.9) | data formatting | bytes 524288 | tf_op args[4]
  3.2 1.0 copy.12.w_ref
  4.3 111.7 %shard_map.55 = bf16[256,512]{1,0:T(8,128)(2,1)} custom-call(bf16[1024,2048]{1,0:T(8,128)(2,1)} %p_ref.1, f32[1024,1]{1,0:T(8,128)} %copy.12.w_ref, bf16[256,512]{1,0:T(8,128)(2,1)} %bitcast.3), custom_call_target="tpu_custom_call" | custom-call | tf_op jit(solution)/shard_map/pallas_call | solution.py:224
  116.0 1.8 %copy.13 = bf16[512,256]{1,0:T(8,128)(2,1)} copy(bf16[512,256]{0,1:T(8,128)(2,1)} %bitcast.4) | data formatting | bytes 524288 | tf_op jit(solution)/shard_map/transpose | solution.py:245

commit v2 on v1

--- a/solution.py
+++ b/solution.py
@@ -19,7 +19,7 @@
     return t
 
 
-def kernel(R, Z, n, p_ref, w_ref, f_ref, out_ref, s2, part, r0, rt, rz, cx, x0, xs, ot, send_sem, recv_sem):
+def kernel(R, Z, n, labels_ref, gain_ref, index_ref, p_hbm, f_ref, out_ref, p_ref, ft, s2, part, r0, rt, rz, cx, x0, xs, ot, send_sem, recv_sem, load_sem):
     bits = R.bit_length() - 1
     blocks = n // LANES
     half = blocks // 2
@@ -76,6 +76,16 @@
             src_ref=ref, dst_ref=ref, send_sem=send_sem.at[0],
             recv_sem=recv_sem.at[slot(key)], device_id=partner, device_id_type=MESH).wait_recv()
 
+    rows_at_once = LANES
+    loads = p_ref.shape[0] // rows_at_once
+
+    def load(i):
+        rows = pl.ds(i * rows_at_once, rows_at_once)
+        return pltpu.make_async_copy(p_hbm.at[rows, :], p_ref.at[rows, :], load_sem.at[i])
+
+    for i in range(loads):
+        load(i).start()
+
     barrier = pltpu.get_barrier_semaphore()
     peers = [((row + k) % R, col) for k in range(1, R)]
     peers += [(row, ((z + k) % Z) * 2 + h) for k in range(1, Z)] + [partner]
@@ -89,14 +99,26 @@
     def slab_at(r):
         return pl.ds(pl.multiple_of(r * mine_cols, mine_cols), mine_cols)
 
+    ft[...] = f_ref[...].T
     for k in range(1, R):
         to = (row + k) % R
-        send(f_ref.at[slab_at(to), :], x0.at[:, columns_at(row)], (to, col), ("field", k))
-    x0[:, columns_at(row)] = f_ref[slab_at(row), :]
-
-    scaled = (p_ref[...].astype(jnp.float32) * w_ref[...]).astype(jnp.bfloat16)
-    s2[:, :n] = scaled
-    s2[:, n:] = scaled[:, : width - LANES]
+        send(ft.at[slab_at(to), :], x0.at[:, columns_at(row)], (to, col), ("field", k))
+    x0[:, columns_at(row)] = ft[slab_at(row), :]
+
+    labels = labels_ref[...]
+    weight = jnp.zeros(labels.shape, jnp.float32)
+    for region in range(gain_ref.shape[0]):
+        weight = jnp.where(labels == region, gain_ref[region] + index_ref[region], weight)
+    for i in range(loads):
+        rows = pl.ds(i * rows_at_once, rows_at_once)
+        along = jnp.broadcast_to(weight[i : i + 1, :], (LANES, LANES)).T
+        load(i).wait()
+        for c in range(n // LANES):
+            columns = pl.ds(c * LANES, LANES)
+            scaled = (p_ref[rows, columns].astype(jnp.float32) * along).astype(jnp.bfloat16)
+            s2[rows, columns] = scaled
+            if c * LANES < width - LANES:
+                s2[rows, pl.ds(n + c * LANES, LANES)] = scaled
 
     order = sorted(range(R), key=lambda g: (lowest_bit(g) if g else bits, -g))
     pair = 2 * LANES
@@ -152,30 +174,50 @@
             send(view, view, (flip(row, t), col), ("spread", g | (1 << t), key_j))
         send(view, view, partner, ("spread_core", mirrored(g), key_j))
 
-    mine = window_of(strip_of(row, z, h))
-    for j in range(Z - 1):
-        send(mine, mine, (row, z_of(j) * 2 + h), ("spread", 0, j + 1))
-    for j in range(Z):
-        for g in range(R):
-            low = lowest_bit(g) if g else bits
-            source_z = (z + Z - j) % Z
-            strip = strip_of(row_of(g), source_z, h)
-            if g or j:
-                arrived(window_of(strip), ("spread", g, j))
-            spread(g, strip, j)
-    for j in range(Z):
-        for g in range(R):
-            strip = strip_of(row_of(g), (z + Z - j) % Z, 1 - h)
-            arrived(window_of(strip), ("spread_core", g, j))
-
-    @pl.loop(0, blocks)
-    def _(i):
+    def mirror_block(i):
         rows = pl.ds(pl.multiple_of(i * LANES, LANES), LANES)
-
         for d in range(1, half):
             to = pl.multiple_of(((i + d) % blocks) * LANES, LANES)
             block = cx[rows, pl.ds(pl.multiple_of((i + d) * LANES, LANES), LANES)]
             cx[pl.ds(to, LANES), rows] = block.T
+
+    def source_z(j):
+        return (z + Z - j) % Z
+
+    mine = window_of(strip_of(row, z, h))
+    for j in range(Z - 1):
+        send(mine, mine, (row, z_of(j) * 2 + h), ("spread", 0, j + 1))
+
+    def tick(at):
+        g, j = at
+        low = lowest_bit(g) if g else bits
+        return j + bin(g).count("1") + (low == 0), -low
+
+    per_chip = 2 * depth == LANES
+    schedule = sorted(((g, j) for g in range(R) for j in range(Z)), key=tick)
+    lag = 3
+    here, there = set(), set()
+    for step in range(len(schedule) + lag):
+        touched = []
+        if step < len(schedule):
+            g, j = schedule[step]
+            strip = strip_of(row_of(g), source_z(j), h)
+            if g or j:
+                arrived(window_of(strip), ("spread", g, j))
+            spread(g, strip, j)
+            here.add((g, j))
+            touched.append((g, j))
+        if step >= lag:
+            g, j = schedule[step - lag]
+            g = mirrored(g)
+            arrived(window_of(strip_of(row_of(g), source_z(j), 1 - h)), ("spread_core", g, j))
+            there.add((g, j))
+            touched.append((g, j))
+        for g, j in touched:
+            if per_chip and (g, j) in here and (g, j) in there:
+                mirror_block(row_of(g) * Z + source_z(j))
+    if not per_chip:
+        pl.loop(0, blocks)(mirror_block)
 
     for i in range(half, blocks):
         rows = pl.ds(i * LANES, LANES)
@@ -210,11 +252,6 @@
 
 
 def on_device(R, Z, mode_profiles, region_labels, gain_table, index_table, field_in):
-    table = gain_table + index_table
-    regions = jnp.arange(table.shape[0], dtype=jnp.int32)
-    weight = jnp.sum(
-        jnp.where(region_labels[:, None] == regions[None, :], table[None, :], 0.0), axis=1, keepdims=True
-    )
     points, n = mode_profiles.shape
     width = n // 2 + LANES
     depth = n // (R * Z * 2)
@@ -224,9 +261,17 @@
     turned = pl.pallas_call(
         functools.partial(kernel, R, Z, n),
         out_shape=jax.ShapeDtypeStruct(field_in.shape[::-1], bf16),
-        in_specs=[pl.BlockSpec(memory_space=pltpu.VMEM)] * 3,
+        in_specs=[
+            pl.BlockSpec(memory_space=pltpu.VMEM),
+            pl.BlockSpec(memory_space=pltpu.SMEM),
+            pl.BlockSpec(memory_space=pltpu.SMEM),
+            pl.BlockSpec(memory_space=pl.ANY),
+            pl.BlockSpec(memory_space=pltpu.VMEM),
+        ],
         out_specs=pl.BlockSpec(memory_space=pltpu.VMEM),
         scratch_shapes=[
+            pltpu.VMEM((points, n), bf16),
+            pltpu.VMEM(field_in.shape[::-1], bf16),
             pltpu.VMEM((points, n + width - LANES), bf16),
             pltpu.VMEM((n, width), bf16),
             pltpu.VMEM((R * Z, depth, width), bf16),
@@ -238,10 +283,11 @@
             pltpu.VMEM(field_in.shape[::-1], bf16),
             pltpu.SemaphoreType.DMA((messages,)),
             pltpu.SemaphoreType.DMA((messages,)),
+            pltpu.SemaphoreType.DMA((points // LANES,)),
         ],
         compiler_params=pltpu.CompilerParams(
             collective_id=0, has_side_effects=True, vmem_limit_bytes=60 * 1024 * 1024),
-    )(mode_profiles, weight, field_in.T)
+    )(region_labels.reshape(-1, LANES), gain_table, index_table, mode_profiles, field_in)
     return turned.T
 
 

time: 118 us -> 92.2 us (0.78)
  the two profiles are of different devices: /device:TPU:9 before, /device:TPU:16 now
where the time goes in v2:
time: 92.2 us; the launch traced here: 92.1 us
  Pallas kernels  90.3 us (98%)
  local copies, waits for them, and re-layouts  1.79 us (2%)
    pallas_call x1, Pallas kernels, on_device(): pl.pallas_call(functools.partial(kernel, R, Z, n), out_shape=jax.ShapeDty...  90.3 us

profile of v2, /device:TPU:16, one launch (start us, length us, event | category | flops | bytes accessed | tf_op | source)
XLA Modules:
  0.0 92.1 jit_solution(2540163277588551324)
XLA Ops:
  0.0 90.3 %shard_map.55 = bf16[256,512]{1,0:T(8,128)(2,1)} custom-call(s32[8,128]{1,0:T(8,128)} %bitcast.3, f32[16]{0:T(128)} %gain_ref.1, f32[16]{0:T(128)} %index_ref.1, bf16[1024,2048]{1,0:T(8,128)(2,1)} %p_hbm.1, bf16[512,256]{1,0:T(8,128)(2,1)} %f_ref.1), custom_call_target="tpu_custom_call" | custom-call | tf_op jit(solution)/shard_map/pallas_call | solution.py:261
  90.3 1.8 %copy.6 = bf16[512,256]{1,0:T(8,128)(2,1)} copy(bf16[512,256]{0,1:T(8,128)(2,1)} %bitcast.2) | data formatting | bytes 524288 | tf_op jit(solution)/shard_map/transpose | solution.py:291

commit v3 on v2

--- a/solution.py
+++ b/solution.py
@@ -91,7 +91,6 @@
     peers += [(row, ((z + k) % Z) * 2 + h) for k in range(1, Z)] + [partner]
     for peer in peers:
         pl.semaphore_signal(barrier, inc=1, device_id=peer, device_id_type=MESH)
-    pl.semaphore_wait(barrier, len(peers))
 
     def columns_at(r):
         return pl.ds(pl.multiple_of(r * row_rows, row_rows), row_rows)
@@ -100,11 +99,6 @@
         return pl.ds(pl.multiple_of(r * mine_cols, mine_cols), mine_cols)
 
     ft[...] = f_ref[...].T
-    for k in range(1, R):
-        to = (row + k) % R
-        send(ft.at[slab_at(to), :], x0.at[:, columns_at(row)], (to, col), ("field", k))
-    x0[:, columns_at(row)] = ft[slab_at(row), :]
-
     labels = labels_ref[...]
     weight = jnp.zeros(labels.shape, jnp.float32)
     for region in range(gain_ref.shape[0]):
@@ -121,29 +115,13 @@
                 s2[rows, pl.ds(n + c * LANES, LANES)] = scaled
 
     order = sorted(range(R), key=lambda g: (lowest_bit(g) if g else bits, -g))
-    pair = 2 * LANES
-    for g in order:
-        r = row_of(g)
-
-        @pl.loop(0, row_rows // pair)
-        def _(q):
-            base = pl.multiple_of(r * row_rows + q * pair, pair)
-            left = p_ref[:, pl.ds(base, pair)].T
-            both = jnp.dot(left, s2[:, pl.ds(base, width + LANES)], preferred_element_type=jnp.float32)
-            part[pl.ds(base, LANES), :] = both[:LANES, :width].astype(jnp.bfloat16)
-            part[pl.ds(base + LANES, LANES), :] = both[LANES:, LANES:].astype(jnp.bfloat16)
-
-        for j in range(Z):
-            send(rows_of(part, strip_of(r, z_of(j), 1 - h)), r0.at[mirrored(g) * Z + j], partner, ("core", mirrored(g), j))
-            ids.setdefault(("core", g, j), len(ids))
-
     stage_slot = {}
     for t in range(bits):
         for g in range(R):
             if g % (2 << t) == 0:
                 stage_slot[t, g] = len(stage_slot)
 
-    for g in order:
+    def reduce_group(g):
         r = row_of(g)
         low = lowest_bit(g) if g else bits
         for j in range(Z):
@@ -166,6 +144,33 @@
                     arrived(rz.at[i], ("z", i))
                     total = total + rz[i].astype(jnp.float32)
                 window_of(strip_of(row, z, h))[...] = total.astype(jnp.bfloat16)
+
+    pair = 2 * LANES
+    waiting = list(order)
+    for at, g in enumerate(order):
+        r = row_of(g)
+
+        @pl.loop(0, row_rows // pair)
+        def _(q):
+            base = pl.multiple_of(r * row_rows + q * pair, pair)
+            left = p_ref[:, pl.ds(base, pair)].T
+            both = jnp.dot(left, s2[:, pl.ds(base, width + LANES)], preferred_element_type=jnp.float32)
+            part[pl.ds(base, LANES), :] = both[:LANES, :width].astype(jnp.bfloat16)
+            part[pl.ds(base + LANES, LANES), :] = both[LANES:, LANES:].astype(jnp.bfloat16)
+
+        if at == 0:
+            pl.semaphore_wait(barrier, len(peers))
+        for j in range(Z):
+            send(rows_of(part, strip_of(r, z_of(j), 1 - h)), r0.at[mirrored(g) * Z + j], partner, ("core", mirrored(g), j))
+        while waiting and order.index(waiting[0]) < at and order.index(mirrored(waiting[0])) <= at:
+            reduce_group(waiting.pop(0))
+    for g in waiting:
+        reduce_group(g)
+
+    for k in range(1, R):
+        to = (row + k) % R
+        send(ft.at[slab_at(to), :], x0.at[:, columns_at(row)], (to, col), ("field", k))
+    x0[:, columns_at(row)] = ft[slab_at(row), :]
 
     def spread(g, strip, key_j):
         low = lowest_bit(g) if g else bits
@@ -226,17 +231,13 @@
 
     for k in range(1, R):
         arrived(x0.at[:, columns_at((row + R - k) % R)], ("field", k))
-    chunk = 4 * LANES
     for index in range(TERMS):
         source = x0 if index == 0 else xs.at[(index + 1) % 2]
         target = xs.at[index % 2]
         scale = 1.0 / (TERMS - index)
 
-        @pl.loop(0, n // chunk)
-        def _(c):
-            columns = pl.ds(pl.multiple_of(c * chunk, chunk), chunk)
-            product = jnp.dot(source[...], cx[:, columns], preferred_element_type=jnp.float32)
-            target[:, columns] = (x0[:, columns].astype(jnp.float32) + scale * product).astype(jnp.bfloat16)
+        product = jnp.dot(source[...], cx[:, :n], preferred_element_type=jnp.float32)
+        target[...] = (x0[...].astype(jnp.float32) + scale * product).astype(jnp.bfloat16)
 
     last = xs.at[(TERMS - 1) % 2]
     for k in range(1, R):

time: 92.2 us -> 83.8 us (0.909)
  Pallas kernels: 90.3 us -> 81.8 us
    pallas_call x1, Pallas kernels: 90.3 us -> 81.8 us  [on_device(): pl.pallas_call(functools.partial(kernel, R, Z, n), out_shape=jax.ShapeDty...]
where the time goes in v3:
time: 83.8 us; the launch traced here: 83.6 us
  Pallas kernels  81.8 us (98%)
  local copies, waits for them, and re-layouts  1.79 us (2%)
    pallas_call x1, Pallas kernels, on_device(): pl.pallas_call(functools.partial(kernel, R, Z, n), out_shape=jax.ShapeDty...  81.8 us
    transpose x1, local copies, waits for them, and re-layouts, on_device(): return turned.T  1.79 us

profile of v3, /device:TPU:16, one launch (start us, length us, event | category | flops | bytes accessed | tf_op | source)
XLA Modules:
  0.0 83.6 jit_solution(635423544211536831)
XLA Ops:
  0.0 81.8 %shard_map.55 = bf16[256,512]{1,0:T(8,128)(2,1)} custom-call(s32[8,128]{1,0:T(8,128)} %bitcast.3, f32[16]{0:T(128)} %gain_ref.1, f32[16]{0:T(128)} %index_ref.1, bf16[1024,2048]{1,0:T(8,128)(2,1)} %p_hbm.1, bf16[512,256]{1,0:T(8,128)(2,1)} %f_ref.1), custom_call_target="tpu_custom_call" | custom-call | tf_op jit(solution)/shard_map/pallas_call | solution.py:262
  81.9 1.8 %copy.6 = bf16[512,256]{1,0:T(8,128)(2,1)} copy(bf16[512,256]{0,1:T(8,128)(2,1)} %bitcast.2) | data formatting | bytes 524288 | tf_op jit(solution)/shard_map/transpose | solution.py:292
